TPU v7x, 32 devices: a whole 2x2x4 slice. The times are simulated.
32 devices in a mesh: group: 2 (over x), replica: 16 (over z, y, core).
Axes of the slice: x: 2, y: 2, z: 4, core: 2. Of those that a mesh axis runs over, the one named last changes fastest.
Arguments:
- tokens: bfloat16 [32, 1024, 768], P(('group', 'replica')), may hold values from -6 to 6
- lengths: int32 [32], P(('group', 'replica')), may hold values from 256 to 1024, as said below
- w_qkv: bfloat16 [768, 2304], P('group'), may hold values from -0.21875 to 0.21875
- w_out: bfloat16 [768, 768], P('group'), may hold values from -4 to 4
- gain_one: bfloat16 [768], P('group'), may hold values from 0.25 to 1.75
- w_in: bfloat16 [768, 2304], P('group'), may hold values from -0.21875 to 0.21875
- w_down: bfloat16 [1152, 768], P('group'), may hold values from -0.1875 to 0.1875
- gain_two: bfloat16 [768], P('group'), may hold values from 0.25 to 1.75
- cotangent: bfloat16 [32, 1024, 768], P(('group', 'replica')), may hold values from -6 to 6
Outputs:
- output: bfloat16 [32, 1024, 768], P(('group', 'replica'))
- grad_tokens: float32 [32, 1024, 768], P(('group', 'replica'))
- grad_qkv: float32 [768, 2304], P('group')
- grad_out: float32 [768, 768], P('group')
- grad_gain_one: float32 [768], P('group')
- grad_in: float32 [768, 2304], P('group')
- grad_down: float32 [1152, 768], P('group')
- grad_gain_two: float32 [768], P('group')
Inputs may be any that keep to these rules, and one draw needn't show every extreme that they name: Slots 0 to lengths - 1 of a sequence hold tokens, the rest are padding; some sequence has exactly 1024 valid slots and some exactly 256.
All inputs are finite; a program needn't handle non-finite values.
Results may differ from a plain program's by a relative error of at most 0.018.
Values may be sent and summed in bfloat16 or wider, within the bound.
No kernel may reach another device: no remote copies, remote signals or barrier semaphores. Data moves between devices by JAX's collectives and lax.ppermute only.
A program may use at most 192 MiB of HBM per device.

v0:
```python
import math

import jax
import jax.numpy as jnp
from jax import lax
from jax.sharding import PartitionSpec as P

HEADS = 12
HEAD_DIM = 64


theta_base = 160000.0
norm_eps = 1e-05


def normed(field, gain):
    center = field - jnp.mean(field, axis=-1, keepdims=True)
    spread = jnp.mean(center * center, axis=-1, keepdims=True)
    return center * lax.rsqrt(spread + norm_eps) * gain


def rotary(field):
    half = HEAD_DIM // 2
    length = field.shape[1]
    freq = jnp.exp(-math.log(theta_base) * 2.0 * jnp.arange(half, dtype=jnp.float32) / HEAD_DIM)
    angle = jnp.arange(length, dtype=jnp.float32)[:, None] * freq[None, :]
    cosine = jnp.cos(angle)
    sine = jnp.sin(angle)
    first = field[..., :half]
    second = field[..., half:]
    return jnp.concatenate(
        [first * cosine - second * sine, second * cosine + first * sine], axis=-1
    )


def rotate_both(query, key_rows):
    return (rotary(query), rotary(key_rows))


def geglu(upward):
    half = upward.shape[1] // 2
    return jax.nn.gelu(upward[:, :half], approximate=False) * upward[:, half:]


def inner(left, right):
    return lax.dot_general(
        left, right, (((0,), (0,)), ((), ())), preferred_element_type=jnp.float32
    )


def outer(left, right):
    return lax.dot_general(
        left, right, (((1,), (1,)), ((), ())), preferred_element_type=jnp.float32
    )


def on_device(tokens, lengths, w_qkv, w_out, gain_one, w_in, w_down, gain_two, cotangent):
    field = tokens[0].astype(jnp.float32)
    length = field.shape[0]
    width = field.shape[1]
    scale = 1.0 / math.sqrt(HEAD_DIM)
    valid = jnp.arange(length, dtype=jnp.int32) < lengths[0]
    qkv_full, out_full, gain_first = (
        lax.all_gather(w_qkv, "group", axis=0, tiled=True),
        lax.all_gather(w_out, "group", axis=0, tiled=True),
        lax.all_gather(gain_one, "group", axis=0, tiled=True),
    )
    in_full, down_full, gain_second = (
        lax.all_gather(w_in, "group", axis=0, tiled=True),
        lax.all_gather(w_down, "group", axis=0, tiled=True),
        lax.all_gather(gain_two, "group", axis=0, tiled=True),
    )
    first_f, first_pull = jax.vjp(normed, field, gain_first.astype(jnp.float32))
    first_in = first_f.astype(jnp.bfloat16)
    merged = jnp.dot(first_in, qkv_full, preferred_element_type=jnp.float32)
    parts = merged.reshape(length, 3, HEADS, HEAD_DIM).transpose(1, 2, 0, 3)
    (query_f, key_f), rotate_pull = jax.vjp(rotate_both, parts[0], parts[1])
    query = query_f.astype(jnp.bfloat16)
    key_rows = key_f.astype(jnp.bfloat16)
    values = parts[2].astype(jnp.bfloat16)

    def masked_scores(head_query, head_keys):
        scores = (
            jnp.einsum("qd,kd->qk", head_query, head_keys, preferred_element_type=jnp.float32)
            * scale
        )
        return jnp.where(valid[None, :], scores, -1e30)

    def forward_head(item):
        head_query, head_keys, head_values = item
        scores = masked_scores(head_query, head_keys)
        top = jnp.max(scores, axis=1, keepdims=True)
        weights = jnp.exp(scores - top)
        total = jnp.sum(weights, axis=1, keepdims=True)
        weights = weights / total
        result = jnp.einsum(
            "qk,kd->qd",
            weights.astype(jnp.bfloat16),
            head_values,
            preferred_element_type=jnp.float32,
        )
        return (result, top[:, 0] + jnp.log(total[:, 0]))

    heads, log_totals = lax.map(forward_head, (query, key_rows, values))
    mixed = heads.transpose(1, 0, 2).reshape(length, width).astype(jnp.bfloat16)
    middle = field + jnp.dot(mixed, out_full, preferred_element_type=jnp.float32)
    second_f, second_pull = jax.vjp(normed, middle, gain_second.astype(jnp.float32))
    second_in = second_f.astype(jnp.bfloat16)
    upward = jnp.dot(second_in, in_full, preferred_element_type=jnp.float32)
    activ_f, activ_pull = jax.vjp(geglu, upward)
    activ = activ_f.astype(jnp.bfloat16)
    result = middle + jnp.dot(activ, down_full, preferred_element_type=jnp.float32)
    output = jnp.where(valid[:, None], result, 0.0).astype(jnp.bfloat16)[None]
    in_back, down_back = (
        lax.all_gather(w_in, "group", axis=0, tiled=True),
        lax.all_gather(w_down, "group", axis=0, tiled=True),
    )
    d_out = jnp.where(valid[:, None], cotangent[0], jnp.zeros((), jnp.bfloat16))
    grad_down = inner(activ, d_out)
    d_activ = outer(d_out, down_back)
    (d_up,) = activ_pull(d_activ)
    d_up = d_up.astype(jnp.bfloat16)
    grad_in = inner(second_in, d_up)
    d_second = outer(d_up, in_back)
    d_middle_norm, grad_gain_two = second_pull(d_second)
    d_middle = d_out.astype(jnp.float32) + d_middle_norm
    qkv_back, out_back = (
        lax.all_gather(w_qkv, "group", axis=0, tiled=True),
        lax.all_gather(w_out, "group", axis=0, tiled=True),
    )
    d_middle_low = d_middle.astype(jnp.bfloat16)
    grad_out = inner(mixed, d_middle_low)
    d_mixed = outer(d_middle_low, out_back).astype(jnp.bfloat16)
    d_heads = d_mixed.reshape(length, HEADS, HEAD_DIM).transpose(1, 0, 2)

    def backward_head(item):
        head_query, head_keys, head_values, head_grad, log_total = item
        scores = masked_scores(head_query, head_keys)
        weights = jnp.where(valid[None, :], jnp.exp(scores - log_total[:, None]), 0.0)
        d_values = jnp.einsum(
            "qk,qd->kd", weights.astype(jnp.bfloat16), head_grad, preferred_element_type=jnp.float32
        )
        d_weights = jnp.einsum(
            "qd,kd->qk", head_grad, head_values, preferred_element_type=jnp.float32
        )
        d_scores = weights * (d_weights - jnp.sum(weights * d_weights, axis=1, keepdims=True))
        d_scores = d_scores.astype(jnp.bfloat16)
        d_query = (
            jnp.einsum("qk,kd->qd", d_scores, head_keys, preferred_element_type=jnp.float32) * scale
        )
        d_keys = (
            jnp.einsum("qk,qd->kd", d_scores, head_query, preferred_element_type=jnp.float32)
            * scale
        )
        return (d_query, d_keys, d_values)

    d_query_r, d_keys_r, d_values = lax.map(
        backward_head, (query, key_rows, values, d_heads, log_totals)
    )
    d_query, d_keys = rotate_pull((d_query_r, d_keys_r))
    d_merged = (
        jnp.stack([d_query, d_keys, d_values]).transpose(2, 0, 1, 3).reshape(length, 3 * width)
    )
    d_merged = d_merged.astype(jnp.bfloat16)
    grad_qkv = inner(first_in, d_merged)
    d_first = outer(d_merged, qkv_back)
    d_field_norm, grad_gain_one = first_pull(d_first)
    grad_tokens = (d_middle + d_field_norm)[None]
    owned = (
        lax.psum_scatter(
            grad_qkv.astype(jnp.bfloat16), "group", scatter_dimension=0, tiled=True
        ).astype(jnp.float32),
        lax.psum_scatter(
            grad_out.astype(jnp.bfloat16), "group", scatter_dimension=0, tiled=True
        ).astype(jnp.float32),
        lax.psum_scatter(
            grad_gain_one.astype(jnp.bfloat16), "group", scatter_dimension=0, tiled=True
        ).astype(jnp.float32),
        lax.psum_scatter(
            grad_in.astype(jnp.bfloat16), "group", scatter_dimension=0, tiled=True
        ).astype(jnp.float32),
        lax.psum_scatter(
            grad_down.astype(jnp.bfloat16), "group", scatter_dimension=0, tiled=True
        ).astype(jnp.float32),
        lax.psum_scatter(
            grad_gain_two.astype(jnp.bfloat16), "group", scatter_dimension=0, tiled=True
        ).astype(jnp.float32),
    )
    grad_qkv, grad_out, grad_gain_one, grad_in, grad_down, grad_gain_two = lax.psum(
        (owned[0], owned[1], owned[2], owned[3], owned[4], owned[5]), "replica"
    )
    return (
        output,
        grad_tokens,
        grad_qkv,
        grad_out,
        grad_gain_one,
        grad_in,
        grad_down,
        grad_gain_two,
    )


def solution(mesh):
    in_specs = (
        P(("group", "replica"), None, None),
        P(("group", "replica")),
        P("group", None),
        P("group", None),
        P("group"),
        P("group", None),
        P("group", None),
        P("group"),
        P(("group", "replica"), None, None),
    )
    out_specs = (
        P(("group", "replica"), None, None),
        P(("group", "replica"), None, None),
        P("group", None),
        P("group", None),
        P("group"),
        P("group", None),
        P("group", None),
        P("group"),
    )
    return jax.shard_map(
        on_device, mesh=mesh, in_specs=in_specs, out_specs=out_specs, check_vma=False
    )
```

profile of v0, /device:TPU:1, one launch (start us, length us, event | category | flops | bytes accessed | tf_op | source)
XLA Modules:
  0.0 709.5 jit_solution(13327913640068594382)
XLA Ops:
  13.3 3.8 all-gather
  17.7 3.2 all-gather.1
  21.7 2.7 copy.38
  24.3 36.5 %all-gather.7.cloned.1.call-done = bf16[768,2304]{1,0:T(8,128)(2,1)} async-done(((bf16[384,2304]{1,0:T(8,128)(2,1)}), bf16[768,2304]{1,0:T(8,128)(2,1)}) %all-gather.7.cloned.1.call-update) | async-done | bytes 3538960 | tf_op jit(solution)/shard_map/all_gather | solution.py:64
  60.8 5.7 copy.32
  66.6 6.1 convolution_bitcast_fusion
  77.8 4.1 copy.34
  81.9 2.7 copy.35
  84.6 4.2 copy.36
  88.9 109.5 %while.30 = (s32[]{:T(128)}, bf16[12,1024,64]{1,2,0:T(8,128)(2,1)S(1)}, f32[12,1024]{1,0:T(8,128)S(1)}, bf16[12,1024,64]{2,1,0:T(8,128)(2,1)}, bf16[12,1024,64]{...) while((s32[]{:T(128)}, bf16[12,1024,64]{1,2,0:T(8,128)(2,1)S(1)}, ...), condition=%wide.region_5.6_spmd.clone.clone, body=%wide.region_2.5_spmd.clone.sunk.clone | while | flops 281018368 | bytes 30455920 | solution.py:104
  94.4 4.0 fusion.151
  104.0 3.5 fusion.151
  113.0 3.5 fusion.151
  122.1 3.5 fusion.151
  131.1 3.5 fusion.151
  140.2 3.5 fusion.151
  149.2 3.5 fusion.151
  158.3 3.5 fusion.151
  167.3 3.5 fusion.151
  176.3 3.5 fusion.151
  185.4 3.5 fusion.151
  194.4 3.5 fusion.151
  198.4 2.8 fusion.97
  202.9 10.6 %fusion.93 = f32[1024,2304]{1,0:T(8,128)} fusion(bf16[768,2304]{1,0:T(8,128)(2,1)} %all-gather.11.cloned.1.call-done, f32[1024,768]{0,1:T(8,128)} %copy-done.10, f32[768]{0:T(1024)S(1)} %reshape.203, f32[1024]{0:T(1024)S(1)} %fusion.88, f32[1024]{0:T(1024)S(1)} %broadcast_multiply_fusion), kind=kOutput, calls=%fused_computation.160 | convolution fusion | flops 3627024384 | bytes 16133120 | tf_op jit(solution)/shard_map/dot_general | solution.py:109
  213.5 15.2 %fusion.76 = (f32[1024,1152]{1,0:T(8,128)}, f32[1024,1152]{1,0:T(8,128)S(1)}, f32[1024,1152]{1,0:T(8,128)S(1)}) fusion(f32[1024,2304]{1,0:T(8,128)} %fusion.93, bf16[1152,768]{1,0:T(8,128)(2,1)} %all-gather.13.cloned.1.call-done, bf16[1,1024,768]{1,2,0:T(8,128)(2,1)S(1)} %copy-done.8, pred[1024]{0:T(1024)(128)(4,1)S(1)} %iota_compare_fusion.2), kind=kOutput, calls=%fused_computation.130 | convolution fusion | flops 1889402880 | bytes 22217728 | tf_op jit(solution)/shard_map/dot_general | solution.py:52
  228.7 3.5 multiply_add_fusion
  232.2 9.0 %multiply_reduce_fusion.1 = (bf16[768]{0:T(1024)(128)(2,1)S(1)}, f32[1024]{0:T(1024)S(1)}, f32[1024,768]{0,1:T(8,128)S(1)}) fusion(f32[1024,768]{0,1:T(8,128)S(1)} %copy-done.11, f32[1024]{0:T(1024)S(1)} %fusion.88, f32[1024]{0:T(1024)S(1)} %broadcast_multiply_fusion, f32[768]{0:T(1024)S(1)} %reshape.203, ...), kind=kOutput, calls=%fused_computation.104 | convolution fusion | flops 3634100480 | bytes 19284480 | tf_op jit(solution)/shard_map/dot_general | solution.py:52
  244.8 2.5 convolution_convert_fusion.4
  247.3 5.0 convolution_convert_fusion.2
  252.5 3.8 convolution_convert_fusion.3
  256.3 4.3 copy.39
  260.6 9.5 %convolution_convert_fusion = bf16[768,2304]{1,0:T(8,128)(2,1)} fusion(f32[1024,1152]{1,0:T(8,128)} %copy-done.15, f32[1024,1152]{1,0:T(8,128)} %get-tuple-element.243, f32[1024,768]{0,1:T(8,128)S(1)} %copy-done.12, f32[768]{0:T(1024)S(1)} %reshape.203, f32[1024]{0:T(1024)S(1)} %fusion.88, f32[1024]{0:T(1024)S(1)} %broadcast_multiply_fusion), kind=kOutput, calls=%fused_computation.61 | convolution fusion | flops 3633512448 | bytes 16133120 | tf_op jit(solution)/shard_map/dot_general | solution.py:46
  271.5 152.0 %while.31 = (s32[]{:T(128)}, f32[12,1024,64]{1,2,0:T(8,128)}, f32[12,1024,64]{1,2,0:T(8,128)}, bf16[12,1024,64]{1,2,0:T(8,128)(2,1)S(1)}, bf16[12,1024,64]{2,1,0...) while((s32[]{:T(128)}, f32[12,1024,64]{1,2,0:T(8,128)}, ...), condition=%wide.region_12.13_spmd.clone.clone, body=%wide.region_10.12_spmd.clone.sunk.clone | while | flops 681705472 | bytes 34106476 | solution.py:157
  274.2 2.7 multiply_reduce_fusion.6
  278.0 2.5 fusion.162
  286.9 2.7 multiply_reduce_fusion.6
  290.7 2.4 fusion.162
  299.5 2.7 multiply_reduce_fusion.6
  303.3 2.4 fusion.162
  312.3 2.7 multiply_reduce_fusion.6
  316.1 2.4 fusion.162
  324.9 2.7 multiply_reduce_fusion.6
  337.5 2.7 multiply_reduce_fusion.6
  341.4 2.4 fusion.162
  350.2 2.7 multiply_reduce_fusion.6
  362.8 2.7 multiply_reduce_fusion.6
  375.5 2.7 multiply_reduce_fusion.6
  379.3 2.4 fusion.162
  388.1 2.7 multiply_reduce_fusion.6
  391.9 2.4 fusion.162
  400.7 2.7 multiply_reduce_fusion.6
  404.5 2.5 fusion.162
  413.3 2.7 multiply_reduce_fusion.6
  417.2 2.4 fusion.162
  423.5 3.8 multiply_add_fusion.4
  430.6 5.6 convolution_convert_fusion.1
  438.1 6.8 fusion.66
  447.3 3.2 add_bitcast_fusion
  450.6 3.9 copy.44
  454.5 5.8 fusion.77
  460.3 2.6 copy.43
  462.9 4.4 all-reduce.9
  467.4 16.9 %reduce-scatter.5.cloned.1.call-done = bf16[384,2304]{1,0:T(8,128)(2,1)} async-done(((bf16[768,2304]{1,0:T(8,128)(2,1)}), bf16[384,2304]{1,0:T(8,128)(2,1)}) %reduce-scatter.5.cloned.1.call-update) | async-done | bytes 1769488 | tf_op jit(solution)/shard_map/reduce_scatter | solution.py:170
  484.3 217.9 %all-reduce.11 = (f32[384,2304]{1,0:T(8,128)}, f32[384,768]{1,0:T(8,128)}, f32[384]{0:T(512)}, f32[384,2304]{1,0:T(8,128)}, f32[576,768]{1,0:T(8,128)}, /*index=5*/f32[384]{0:T(512)}) all-reduce(bf16[384,2304]{1,0:T(8,128)(2,1)} %reduce-scatter.5.cloned.1.call-done, ...), channel_id=1, replica_groups=mesh['group'=2,'replica'=16] {'replica'}, use_global_device_ids=true, to_apply=%region_16.17 | all-reduce | flops 2507520 | bytes 15046656 | tf_op jit(solution)/shard_map/psum | solution.py:189
  (285 shorter events, 188.6 us)
Async XLA Ops:
  7.2 53.7 %all-gather.7.cloned.1.call-start = ((), (), s32[]{:S(2)}) async-start(), calls=%async_computation.4 | async-start | bytes 5308416 | tf_op jit(solution)/shard_map/all_gather | solution.py:64
  7.9 190.5 %all-gather.9.cloned.1.call-start = ((), (), s32[]{:S(2)}) async-start(), calls=%async_computation.5 | async-start | bytes 1769472 | tf_op jit(solution)/shard_map/all_gather | solution.py:65
  8.6 194.3 %all-gather.11.cloned.1.call-start = ((), (), s32[]{:S(2)}) async-start(), calls=%async_computation.6 | async-start | bytes 5308416 | tf_op jit(solution)/shard_map/all_gather | solution.py:69
  9.4 204.1 %all-gather.13.cloned.1.call-start = ((), (), s32[]{:S(2)}) async-start(), calls=%async_computation.7 | async-start | bytes 2654208 | tf_op jit(solution)/shard_map/all_gather | solution.py:70
  10.0 457.4 %reduce-scatter.7.cloned.1.call-start = ((), (), s32[]{:S(2)}) async-start(), calls=%async_computation.9 | async-start | bytes 1769472 | tf_op jit(solution)/shard_map/reduce_scatter | solution.py:173
  10.2 7.5 %copy-start.5 = (bf16[12,1024,64]{1,2,0:T(8,128)(2,1)}, bf16[12,1024,64]{1,2,0:T(8,128)(2,1)S(1)}, u32[]{:S(2)}) copy-start(bf16[12,1024,64]{1,2,0:T(8,128)(2,1)S(1)} %fusion.96) | copy-start | bytes 4718596
  10.2 3.1 copy-start.31
  12.5 185.9 %copy-start.1 = (bf16[1,1024,768]{1,2,0:T(8,128)(2,1)}, bf16[1,1024,768]{1,2,0:T(8,128)(2,1)S(1)}, u32[]{:S(2)}) copy-start(bf16[1,1024,768]{1,2,0:T(8,128)(2,1)S(1)} %copy.31) | copy-start | bytes 4718596
  12.5 5.2 copy-start.32
  12.8 53.7 %copy-start.23 = (f32[1024]{0:T(1024)}, f32[1024]{0:T(1024)S(1)}, u32[]{:S(2)}) copy-start(f32[1024]{0:T(1024)S(1)} %broadcast_multiply_fusion.1) | copy-start | bytes 12292
  13.3 3.8 copy-start.29
  13.3 53.3 %copy-start.27 = (f32[1024]{0:T(1024)}, f32[1024]{0:T(1024)S(1)}, u32[]{:S(2)}) copy-start(f32[1024]{0:T(1024)S(1)} %fusion.87) | copy-start | bytes 12292
  17.1 49.4 %copy-start.25 = (f32[768]{0:T(1024)}, f32[768]{0:T(1024)S(1)}, u32[]{:S(2)}) copy-start(f32[768]{0:T(1024)S(1)} %reshape.202) | copy-start | bytes 9220
  17.7 57.5 %copy-start.19 = (f32[1024,32]{0,1:T(8,128)}, f32[1024,32]{0,1:T(8,128)S(1)}, u32[]{:S(2)}) copy-start(f32[1024,32]{0,1:T(8,128)S(1)} %get-tuple-element.267) | copy-start | bytes 393220
  17.7 57.5 %copy-start.21 = (f32[1024,32]{0,1:T(8,128)}, f32[1024,32]{0,1:T(8,128)S(1)}, u32[]{:S(2)}) copy-start(f32[1024,32]{0,1:T(8,128)S(1)} %get-tuple-element.268) | copy-start | bytes 393220
  84.6 4.2 copy-start.7
  91.3 2.1 copy-start
  100.9 2.1 copy-start
  109.9 2.1 copy-start
  119.0 2.1 copy-start
  128.0 2.1 copy-start
  137.0 2.1 copy-start
  146.1 2.1 copy-start
  155.2 2.1 copy-start
  164.2 2.1 copy-start
  173.2 2.1 copy-start
  182.3 2.1 copy-start
  191.3 2.1 copy-start
  201.2 1.7 copy-start.10
  202.9 10.6 %copy-start.8 = (bf16[1,1024,768]{1,2,0:T(8,128)(2,1)S(1)}, bf16[1,1024,768]{1,2,0:T(8,128)(2,1)}, u32[]{:S(2)}) copy-start(bf16[1,1024,768]{1,2,0:T(8,128)(2,1)} %copy.38) | copy-start | bytes 4718596
  213.5 15.2 %copy-start.14 = (f32[1024,2304]{1,0:T(8,128)S(1)}, f32[1024,2304]{1,0:T(8,128)}, u32[]{:S(2)}) copy-start(f32[1024,2304]{1,0:T(8,128)} %fusion.93) | copy-start | bytes 28311556
  228.7 3.5 copy-start.11
  232.2 9.0 %copy-start.15 = (f32[1024,1152]{1,0:T(8,128)}, f32[1024,1152]{1,0:T(8,128)S(1)}, u32[]{:S(2)}) copy-start(f32[1024,1152]{1,0:T(8,128)S(1)} %get-tuple-element.249) | copy-start | bytes 14155780
  242.0 1.7 copy-start.3
  243.7 1.1 copy-start.17
  247.3 220.1 %reduce-scatter.11.cloned.1.call-start = ((), (), s32[]{:S(2)}) async-start(), calls=%async_computation.11 | async-start | bytes 2654208 | tf_op jit(solution)/shard_map/reduce_scatter | solution.py:182
  247.3 5.2 copy-start.18
  252.4 215.0 %reduce-scatter.9.cloned.1.call-start = ((), (), s32[]{:S(2)}) async-start(), calls=%async_computation.10 | async-start | bytes 5308416 | tf_op jit(solution)/shard_map/reduce_scatter | solution.py:179
  256.3 4.3 copy-start.12
  270.1 1.4 copy-start.6
  270.1 214.1 %reduce-scatter.5.cloned.1.call-start = ((), (), s32[]{:S(2)}) async-start(), calls=%async_computation.8 | async-start | bytes 5308416 | tf_op jit(solution)/shard_map/reduce_scatter | solution.py:170
  271.5 152.0 %copy-start.20 = (f32[1024,32]{0,1:T(8,128)S(1)}, f32[1024,32]{0,1:T(8,128)}, u32[]{:S(2)}) copy-start(f32[1024,32]{0,1:T(8,128)} %copy-done.19) | copy-start | bytes 393220
  271.5 152.0 %copy-start.22 = (f32[1024,32]{0,1:T(8,128)S(1)}, f32[1024,32]{0,1:T(8,128)}, u32[]{:S(2)}) copy-start(f32[1024,32]{0,1:T(8,128)} %copy-done.21) | copy-start | bytes 393220
  427.8 2.8 copy-start.2
  427.9 2.8 copy-start.24
  427.9 2.8 copy-start.26
  427.9 2.8 copy-start.28
  428.5 2.2 copy-start.16
  436.2 0.7 copy-start.33
  438.1 6.9 copy-start.30
  445.0 1.9 copy-start.4
  445.0 2.3 copy-start.9
  450.6 3.9 copy-start.13
Sparse Core Ops, SparseCore 0:
  9.5 51.2 all-gather.6
  62.4 22.7 all-gather.8
  86.7 49.3 all-gather.10
  137.5 29.3 all-gather.12
  247.4 21.8 reduce-scatter.6
  272.0 28.3 reduce-scatter.10
  303.2 47.7 reduce-scatter.8
  436.4 47.8 reduce-scatter.4
where the time goes:
time: 722 us; the launch traced here: 709 us
  matrix products  276 us (38%)
  blocking collectives  229 us (32%)
  local copies, waits for them, and re-layouts  70.6 us (10%)
  other arithmetic  59.4 us (8%)
  waiting for transfers between devices  56 us (8%)
  between operations  16.4 us (2%)
    psum x1, blocking collectives, on_device(): lax.psum((owned[0], owned[1], owned[2], owned[3], owned[4], owned[5]), 'r...  218 us
    dot_general x24, matrix products, masked_scores(): jnp.einsum('qd,kd->qk', head_query, head_keys, preferred_element_type=jnp...  53.5 us
    dot_general x12, matrix products, forward_head(): jnp.einsum('qk,kd->qd', weights.astype(jnp.bfloat16), head_values, prefer...  42.2 us
    all_gather x1, waiting for transfers between devices, on_device(): lax.all_gather(w_qkv, 'group', axis=0, tiled=True)  36.5 us
    dot_general x4, matrix products, outer(): lax.dot_general(left, right, (((1,), (1,)), ((), ())), preferred_element_...  34.8 us
    unnamed x76, local copies, waits for them, and re-layouts  31.7 us
    dot_general x12, matrix products, backward_head(): jnp.einsum('qk,qd->kd', d_scores, head_query, preferred_element_type=jnp....  29.3 us
    dot_general x12, matrix products, backward_head(): jnp.einsum('qk,kd->qd', d_scores, head_keys, preferred_element_type=jnp.f...  26.4 us
  transfers between devices with their start and end apart: 8, of which 2 were waited for; matrix products, arithmetic and copies ran while one was open for 48% of the time, Pallas kernels for 0%

commit v1 on v0

--- a/solution.py
+++ b/solution.py
@@ -54,22 +54,99 @@
     )
 
 
+def swap_replica(field, bit):
+    count = lax.axis_size("replica")
+    return lax.ppermute(field, "replica", [(i, i ^ bit) for i in range(count)])
+
+
+def swap_group(field):
+    return lax.ppermute(field, "group", [(0, 1), (1, 0)])
+
+
+def pick(field, index, axis):
+    size = field.shape[axis] // 2
+    return lax.dynamic_slice_in_dim(field, index * size, size, axis)
+
+
+def in_order(mine, other, index, axis):
+    return jnp.where(
+        index == 0,
+        jnp.concatenate([mine, other], axis=axis),
+        jnp.concatenate([other, mine], axis=axis),
+    )
+
+
+def add_low(left, right):
+    return (left.astype(jnp.float32) + right.astype(jnp.float32)).astype(jnp.bfloat16)
+
+
+def other_rows(send, core):
+    fetched = swap_group(send)
+    return fetched, swap_replica(fetched, 1)
+
+
+def reduce_unit(send, keep, group, replica):
+    count = lax.axis_size("replica")
+    total = add_low(keep, swap_replica(send, 1))
+    total = add_low(pick(total, group, 0), swap_group(pick(total, 1 - group, 0)))[0]
+    split = []
+    bit = 2
+    while bit < count:
+        at = (replica // bit) % 2
+        if total.shape[0] % 32 == 0:
+            total = add_low(pick(total, at, 0), swap_replica(pick(total, 1 - at, 0), bit))
+            split.append((bit, at))
+        else:
+            total = add_low(total, swap_replica(total, bit))
+        bit *= 2
+    for bit, at in reversed(split):
+        total = in_order(total, swap_replica(total, bit), at, 0)
+    return total, swap_replica(total, 1)
+
+
 def on_device(tokens, lengths, w_qkv, w_out, gain_one, w_in, w_down, gain_two, cotangent):
     field = tokens[0].astype(jnp.float32)
     length = field.shape[0]
     width = field.shape[1]
     scale = 1.0 / math.sqrt(HEAD_DIM)
     valid = jnp.arange(length, dtype=jnp.int32) < lengths[0]
-    qkv_full, out_full, gain_first = (
-        lax.all_gather(w_qkv, "group", axis=0, tiled=True),
-        lax.all_gather(w_out, "group", axis=0, tiled=True),
-        lax.all_gather(gain_one, "group", axis=0, tiled=True),
-    )
-    in_full, down_full, gain_second = (
-        lax.all_gather(w_in, "group", axis=0, tiled=True),
-        lax.all_gather(w_down, "group", axis=0, tiled=True),
-        lax.all_gather(gain_two, "group", axis=0, tiled=True),
-    )
+    group = lax.axis_index("group")
+    replica = lax.axis_index("replica")
+    core = replica % 2
+    gain_rows = jnp.zeros((16, w_qkv.shape[1] // 2), jnp.bfloat16)
+    gain_rows = lax.dynamic_update_slice(gain_rows, gain_one[None], (0, 0))
+    qkv_send = jnp.concatenate([pick(w_qkv, core, 1), gain_rows], axis=0)
+    rest_rows = jnp.zeros((16, w_out.shape[1] // 2), jnp.bfloat16)
+    rest_rows = lax.dynamic_update_slice(rest_rows, gain_two[None], (0, 0))
+    wide = w_out.shape[1] // 2
+    in_half = pick(w_in, core, 1)
+    rest_send = jnp.concatenate(
+        [pick(w_out, core, 1), pick(w_down, core, 1)]
+        + [in_half[:, i * wide : (i + 1) * wide] for i in range(3)]
+        + [rest_rows],
+        axis=0,
+    )
+    qkv_parts = other_rows(qkv_send, core)
+    rest_parts = other_rows(rest_send, core)
+    n_own = w_qkv.shape[0]
+    n_down = w_down.shape[0]
+    cut = [0, n_own, n_own + n_down, 2 * n_own + n_down, 3 * n_own + n_down, 4 * n_own + n_down]
+
+    def whole(own, parts):
+        return in_order(own, in_order(parts[0], parts[1], core, 1), group, 0)
+
+    qkv_full = whole(w_qkv, [part[:n_own] for part in qkv_parts])
+    gain_first = in_order(gain_one, qkv_parts[0][n_own, :n_own], group, 0)
+    out_full = whole(w_out, [part[: cut[1]] for part in rest_parts])
+    down_full = whole(w_down, [part[cut[1] : cut[2]] for part in rest_parts])
+    in_full = whole(
+        w_in,
+        [
+            jnp.concatenate([part[cut[i] : cut[i + 1]] for i in (2, 3, 4)], axis=1)
+            for part in rest_parts
+        ],
+    )
+    gain_second = in_order(gain_two, rest_parts[0][cut[5], :n_own], group, 0)
     first_f, first_pull = jax.vjp(normed, field, gain_first.astype(jnp.float32))
     first_in = first_f.astype(jnp.bfloat16)
     merged = jnp.dot(first_in, qkv_full, preferred_element_type=jnp.float32)
@@ -111,26 +188,18 @@
     activ = activ_f.astype(jnp.bfloat16)
     result = middle + jnp.dot(activ, down_full, preferred_element_type=jnp.float32)
     output = jnp.where(valid[:, None], result, 0.0).astype(jnp.bfloat16)[None]
-    in_back, down_back = (
-        lax.all_gather(w_in, "group", axis=0, tiled=True),
-        lax.all_gather(w_down, "group", axis=0, tiled=True),
-    )
     d_out = jnp.where(valid[:, None], cotangent[0], jnp.zeros((), jnp.bfloat16))
     grad_down = inner(activ, d_out)
-    d_activ = outer(d_out, down_back)
+    d_activ = outer(d_out, down_full)
     (d_up,) = activ_pull(d_activ)
     d_up = d_up.astype(jnp.bfloat16)
     grad_in = inner(second_in, d_up)
-    d_second = outer(d_up, in_back)
+    d_second = outer(d_up, in_full)
     d_middle_norm, grad_gain_two = second_pull(d_second)
     d_middle = d_out.astype(jnp.float32) + d_middle_norm
-    qkv_back, out_back = (
-        lax.all_gather(w_qkv, "group", axis=0, tiled=True),
-        lax.all_gather(w_out, "group", axis=0, tiled=True),
-    )
     d_middle_low = d_middle.astype(jnp.bfloat16)
     grad_out = inner(mixed, d_middle_low)
-    d_mixed = outer(d_middle_low, out_back).astype(jnp.bfloat16)
+    d_mixed = outer(d_middle_low, out_full).astype(jnp.bfloat16)
     d_heads = d_mixed.reshape(length, HEADS, HEAD_DIM).transpose(1, 0, 2)
 
     def backward_head(item):
@@ -163,41 +232,63 @@
     )
     d_merged = d_merged.astype(jnp.bfloat16)
     grad_qkv = inner(first_in, d_merged)
-    d_first = outer(d_merged, qkv_back)
+    d_first = outer(d_merged, qkv_full)
     d_field_norm, grad_gain_one = first_pull(d_first)
     grad_tokens = (d_middle + d_field_norm)[None]
-    owned = (
-        lax.psum_scatter(
-            grad_qkv.astype(jnp.bfloat16), "group", scatter_dimension=0, tiled=True
-        ).astype(jnp.float32),
-        lax.psum_scatter(
-            grad_out.astype(jnp.bfloat16), "group", scatter_dimension=0, tiled=True
-        ).astype(jnp.float32),
-        lax.psum_scatter(
-            grad_gain_one.astype(jnp.bfloat16), "group", scatter_dimension=0, tiled=True
-        ).astype(jnp.float32),
-        lax.psum_scatter(
-            grad_in.astype(jnp.bfloat16), "group", scatter_dimension=0, tiled=True
-        ).astype(jnp.float32),
-        lax.psum_scatter(
-            grad_down.astype(jnp.bfloat16), "group", scatter_dimension=0, tiled=True
-        ).astype(jnp.float32),
-        lax.psum_scatter(
-            grad_gain_two.astype(jnp.bfloat16), "group", scatter_dimension=0, tiled=True
-        ).astype(jnp.float32),
-    )
-    grad_qkv, grad_out, grad_gain_one, grad_in, grad_down, grad_gain_two = lax.psum(
-        (owned[0], owned[1], owned[2], owned[3], owned[4], owned[5]), "replica"
-    )
+    def unit_of(fields):
+        halves = []
+        for half in (1 - core, core):
+            parts = []
+            for field in fields:
+                part = pick(field.astype(jnp.bfloat16), half, 1)
+                rows = part.shape[0] // 2
+                for i in range(part.shape[1] // wide):
+                    parts.append(part[:, i * wide : (i + 1) * wide].reshape(2, rows, wide))
+            used = sum(part.shape[1] for part in parts)
+            filled = -(-used // 128) * 128
+            if filled > used:
+                parts.append(jnp.zeros((2, filled - used, wide), jnp.bfloat16))
+            halves.append(jnp.concatenate(parts, axis=1))
+        return halves
+
+    def gain_unit(field):
+        return jnp.zeros((2 * n_own, 2 * wide), jnp.float32).at[:2, :n_own].set(field.reshape(2, n_own))
+
+    def spread(result, fields):
+        outs = []
+        at = 0
+        for field in fields:
+            rows = field.shape[0] // 2
+            count = field.shape[1] // 2 // wide
+            sides = []
+            for side in result:
+                sides.append(
+                    jnp.concatenate(
+                        [side[at + i * rows : at + (i + 1) * rows] for i in range(count)], axis=1
+                    )
+                )
+            outs.append(in_order(sides[0], sides[1], core, 1).astype(jnp.float32))
+            at += rows * count
+        return outs
+
+    early = [grad_down, grad_in, grad_out]
+    early_sum = reduce_unit(*unit_of(early), group, replica)
+    late = [grad_qkv]
+    late_sum = reduce_unit(*unit_of(late), group, replica)
+    grad_down, grad_in, grad_out = spread(early_sum, early)
+    (grad_qkv,) = spread(late_sum, late)
+    gains = jnp.stack([grad_gain_one, grad_gain_two])
+    gains = lax.psum(gains, ("group", "replica"))
+    gains = lax.dynamic_slice_in_dim(gains, group * n_own, n_own, 1)
     return (
         output,
         grad_tokens,
         grad_qkv,
         grad_out,
-        grad_gain_one,
+        gains[0],
         grad_in,
         grad_down,
-        grad_gain_two,
+        gains[1],
     )
 
 

time: 722 us -> 815 us (1.13)
  blocking collectives: 229 us -> 47.6 us
  local copies, waits for them, and re-layouts: 70.6 us -> 241 us
  waiting for transfers between devices: 56 us -> 104 us
  other arithmetic: 59.4 us -> 102 us
  starting transfers between devices: 0.31 us -> 31.5 us
  between operations: 16.4 us -> 2.8 us
    psum x1, blocking collectives: 218 us -> 47.6 us  [on_device(): gains = lax.psum(gains, ('group', 'replica'))]
    ppermute x0 -> x22, waiting for transfers between devices: none -> 104 us  [the longest x4 69 us: swap_group(): return lax.ppermute(field, 'group', [(0, 1), (1, 0)])]
    unnamed x76 -> x179, local copies, waits for them, and re-layouts: 31.7 us -> 93.2 us
    all_gather x4 -> x0, waiting for transfers between devices: 36.5 us -> none  [the longest x1 36.5 us: on_device(): lax.all_gather(w_qkv, 'group', axis=0, tiled=True)]
    reshape x0 -> x18, local copies, waits for them, and re-layouts: none -> 33.3 us  [the longest x16 33.3 us: unit_of(): parts.append(part[:, i * wide:(i + 1) * wide].reshape(2, rows, wide))]
    ppermute x0 -> x22, starting transfers between devices: none -> 31.5 us  [the longest x18 26.8 us: swap_replica(): return lax.ppermute(field, 'replica', [(i, i ^ bit) for i in range(count)])]
    concatenate x0 -> x10, local copies, waits for them, and re-layouts: none -> 22.4 us  [the longest x2 14 us: unit_of(): halves.append(jnp.concatenate(parts, axis=1))]
    convert_element_type x2 -> x14, other arithmetic: 0.15 us -> 18.4 us  [the longest x10 14.9 us: add_low(): (left.astype(jnp.float32) + right.astype(jnp.float32)).astype(jnp.bfloat16)]
  transfers between devices with their start and end apart: 8 -> 22, of which waited for: 2 -> 8; matrix products, arithmetic and copies ran while one was open for 48% -> 36% of each run, Pallas kernels for 0% -> 0%
where the time goes in v1:
time: 815 us; the launch traced here: 799 us
  matrix products  270 us (33%)
  local copies, waits for them, and re-layouts  241 us (30%)
  waiting for transfers between devices  104 us (13%)
  other arithmetic  102 us (13%)
  blocking collectives  47.6 us (6%)
  starting transfers between devices  31.5 us (4%)
    unnamed x179, local copies, waits for them, and re-layouts  93.2 us
    ppermute x4, waiting for transfers between devices, swap_group(): return lax.ppermute(field, 'group', [(0, 1), (1, 0)])  69 us
    dot_general x24, matrix products, masked_scores(): jnp.einsum('qd,kd->qk', head_query, head_keys, preferred_element_type=jnp...  53.4 us
    psum x1, blocking collectives, on_device(): gains = lax.psum(gains, ('group', 'replica'))  47.6 us
    dot_general x12, matrix products, forward_head(): jnp.einsum('qk,kd->qd', weights.astype(jnp.bfloat16), head_values, prefer...  41.5 us
    dot_general x4, matrix products, outer(): lax.dot_general(left, right, (((1,), (1,)), ((), ())), preferred_element_...  38.9 us
    ppermute x18, waiting for transfers between devices, swap_replica(): return lax.ppermute(field, 'replica', [(i, i ^ bit) for i in range(count)])  34.6 us
    reshape x16, local copies, waits for them, and re-layouts, unit_of(): parts.append(part[:, i * wide:(i + 1) * wide].reshape(2, rows, wide))  33.3 us
  transfers between devices with their start and end apart: 22, of which 8 were waited for; matrix products, arithmetic and copies ran while one was open for 36% of the time, Pallas kernels for 0%

profile of v1, /device:TPU:1, one launch (start us, length us, event | category | flops | bytes accessed | tf_op | source)
XLA Modules:
  0.0 799.1 jit_solution(9865017861474288771)
XLA Ops:
  11.8 4.3 copy.179
  18.3 3.9 copy.195
  34.1 27.3 %collective-permute-done.2 = bf16[2128,384]{1,0:T(8,128)(2,1)} collective-permute-done((bf16[2128,384]{1,0:T(8,128)(2,1)}, bf16[2128,384]{1,0:T(8,128)(2,1)}, u32[]{:S(2)}, u32[]{:S(2)}) %collective-permute-start.2) | collective-permute-done | bytes 1634336 | tf_op jit(solution)/shard_map/ppermute | solution.py:63
  80.1 4.1 convolution_bitcast_fusion
  89.1 3.1 copy.183
  93.8 2.7 copy.182
  96.5 4.3 copy.184
  100.8 123.5 %while.30 = (s32[]{:T(128)}, bf16[12,1024,64]{1,2,0:T(8,128)(2,1)S(1)}, f32[12,1024]{1,0:T(8,128)}, bf16[12,1024,64]{2,1,0:T(8,128)(2,1)}, bf16[12,1024,64]{2,1,...) while((s32[]{:T(128)}, bf16[12,1024,64]{1,2,0:T(8,128)(2,1)S(1)}, ...), condition=%wide.region_5.6_spmd.clone.clone, body=%wide.region_2.5_spmd.clone.sunk.clone | while | flops 281018368 | bytes 30455920 | solution.py:181
  107.6 3.5 fusion.162
  117.9 3.5 fusion.162
  128.2 3.5 fusion.162
  138.5 3.5 fusion.162
  148.8 3.5 fusion.162
  159.1 3.5 fusion.162
  169.4 3.5 fusion.162
  179.7 3.5 fusion.162
  190.0 3.5 fusion.162
  200.2 3.5 fusion.162
  210.5 3.5 fusion.162
  220.8 3.5 fusion.162
  224.3 2.7 fusion.112
  230.3 2.9 fusion.114
  247.4 4.3 fusion.87
  251.7 14.9 %fusion.78 = (f32[1024,1152]{1,0:T(8,128)}, f32[1024,1152]{1,0:T(8,128)S(1)}, f32[1024,1152]{1,0:T(8,128)S(1)}) fusion(f32[1024,2304]{1,0:T(8,128)S(1)} %fusion.87, bf16[576,768]{0,1:T(8,128)(2,1)S(1)} %maximum_select_fusion.6, bf16[576,768]{0,1:T(8,128)(2,1)S(1)} %copy-done.44, pred[]{:T(512)S(6)} %eq.18, bf16[1,1024,768]{1,2,0:T(8,128)(2,1)S(1)} %copy-done.8, ...), kind=kOutput, calls=%fused_computation.147 | convolution fusion | flops 1897365504 | bytes 22217728 | tf_op jit(solution)/shard_map/dot_general | solution.py:52
  266.7 4.5 multiply_add_fusion
  271.2 11.5 %multiply_reduce_fusion.1 = (f32[768]{0:T(1024)}, f32[1024]{0:T(1024)S(1)}, f32[1024,768]{0,1:T(8,128)}) fusion(f32[1024,768]{0,1:T(8,128)S(1)} %copy-done.13, f32[1024]{0:T(1024)S(1)} %fusion.95, f32[1024]{0:T(1024)S(1)} %broadcast_multiply_fusion, f32[768]{0:T(1024)S(1)} %fusion.97, bf16[384,2304]{0,1:T(8,128)(2,1)} %copy-done.32, ...), kind=kOutput, calls=%fused_computation.109 | convolution fusion | flops 3650025728 | bytes 19286016 | tf_op jit(solution)/shard_map/dot_general | solution.py:52
  282.7 9.6 %convolution_convert_fusion = bf16[768,2304]{1,0:T(8,128)(2,1)} fusion(f32[1024,1152]{1,0:T(8,128)} %get-tuple-element.318, f32[1024,1152]{1,0:T(8,128)} %get-tuple-element.312, f32[1024,768]{0,1:T(8,128)S(1)} %copy-done.13, f32[768]{0:T(1024)S(1)} %fusion.97, f32[1024]{0:T(1024)S(1)} %fusion.95, f32[1024]{0:T(1024)S(1)} %broadcast_multiply_fusion), kind=kOutput, calls=%fused_computation.62 | convolution fusion | flops 3633512448 | bytes 16133120 | tf_op jit(solution)/shard_map/dot_general | solution.py:46
  298.0 4.2 copy.203
  302.2 160.5 %while.31 = (s32[]{:T(128)}, f32[12,1024,64]{1,2,0:T(8,128)}, f32[12,1024,64]{1,2,0:T(8,128)}, bf16[12,1024,64]{1,2,0:T(8,128)(2,1)S(1)}, bf16[12,1024,64]{2,1,0...) while((s32[]{:T(128)}, f32[12,1024,64]{1,2,0:T(8,128)}, ...), condition=%wide.region_12.13_spmd.clone.clone, body=%wide.region_10.12_spmd.clone.sunk.clone | while | flops 681705472 | bytes 34106476 | solution.py:226
  305.6 2.7 multiply_reduce_fusion.6
  319.0 2.7 multiply_reduce_fusion.6
  332.3 2.7 multiply_reduce_fusion.6
  345.7 2.7 multiply_reduce_fusion.6
  359.1 2.7 multiply_reduce_fusion.6
  372.4 2.7 multiply_reduce_fusion.6
  385.7 2.7 multiply_reduce_fusion.6
  399.1 2.7 multiply_reduce_fusion.6
  412.4 2.7 multiply_reduce_fusion.6
  425.8 2.7 multiply_reduce_fusion.6
  439.2 2.7 multiply_reduce_fusion.6
  462.8 3.8 multiply_add_fusion.4
  467.8 4.8 convolution_convert_fusion.1
  472.6 2.8 constant_dynamic-slice_fusion.9
  480.8 2.8 pad_maximum_fusion
  483.6 2.8 convolution_convert_fusion.4
  496.1 3.7 convolution_convert_fusion.2
  503.5 6.9 concatenate.218
  523.2 19.9 %collective-permute-done.5 = bf16[1,1152,384]{1,2,0:T(8,128)(2,1)} collective-permute-done((bf16[1,1152,384]{1,2,0:T(8,128)(2,1)}, bf16[1,1152,384]{1,2,0:T(8,128)(2,1)}, u32[]{:S(2)}, u32[]{:S(2)}) %collective-permute-start.5) | collective-permute-done | bytes 884768 | tf_op jit(solution)/shard_map/ppermute | solution.py:63
  559.0 7.1 concatenate.217
  569.9 3.7 add_convert_fusion.1
  581.5 9.8 %fusion.66 = (f32[1024]{0:T(1024)}, f32[1024,768]{0,1:T(8,128)}) fusion(bf16[1,1024,768]{1,2,0:T(8,128)(2,1)S(1)} %copy.176, f32[768]{0:T(1024)S(1)} %copy-done.54, f32[1024]{0:T(1024)S(1)} %copy-done.50, bf16[1024,2304]{0,1:T(8,128)(2,1)} %bitcast.224, bf16[768,2304]{0,1:T(8,128)(2,1)} %copy-done.21), kind=kOutput, calls=%fused_computation.100 | convolution fusion | flops 3627809792 | bytes 12987392 | tf_op jit(solution)/shard_map/dot_general | solution.py:52
  591.7 21.8 %collective-permute-done.14 = bf16[1,2176,384]{1,2,0:T(8,128)(2,1)} collective-permute-done((bf16[1,2176,384]{1,2,0:T(8,128)(2,1)}, bf16[1,2176,384]{1,2,0:T(8,128)(2,1)}, u32[]{:S(2)}, u32[]{:S(2)}) %collective-permute-start.14) | collective-permute-done | bytes 1671200 | tf_op jit(solution)/shard_map/ppermute | solution.py:63
  620.2 7.1 fusion.79
  627.8 5.9 collective-permute-done.10
  644.4 6.6 collective-permute-done.16
  653.6 3.0 maximum_select_fusion.8
  656.5 10.4 %collective-permute-start.12 = (bf16[1152,384]{0,1:T(8,128)(2,1)}, bf16[1152,384]{0,1:T(8,128)(2,1)}, u32[]{:S(2)}, u32[]{:S(2)}) collective-permute-start(bf16[1152,384]{0,1:T(8,128)(2,1)} %maximum_select_fusion.8), channel_id=1, source_target_pairs={{0,1},{1,0},{2,3},{3,2},{4,5},{5,4},{6,7},{7,6},{8,9},{9,8},{10,11... | collective-permute-start | bytes 2654216 | tf_op jit(solution)/shard_map/ppermute | solution.py:59
  667.2 9.3 %collective-permute-done.18 = bf16[272,384]{0,1:T(8,128)(2,1)S(1)} collective-permute-done((bf16[272,384]{0,1:T(8,128)(2,1)S(1)}, bf16[272,384]{0,1:T(8,128)(2,1)S(1)}, u32[]{:S(2)}, u32[]{:S(2)}) %collective-permute-start.18) | collective-permute-done | bytes 208928 | tf_op jit(solution)/shard_map/ppermute | solution.py:59
  677.8 3.3 add_bitcast_fusion
  681.1 3.7 copy.229
  686.3 47.6 %psum.7 = f32[2,768]{1,0:T(2,128)S(1)} all-reduce(f32[2,768]{1,0:T(2,128)S(1)} %pad_maximum_fusion.3), channel_id=1, replica_groups=mesh['group'=2,'replica'=16] {'group','replica'}, use_global_device_ids=true, to_apply=%region_17.18 | all-reduce | flops 1536 | bytes 12288 | tf_op jit(solution)/shard_map/psum | solution.py:281
  748.8 10.8 %collective-permute-done.20 = bf16[1088,384]{1,0:T(8,128)(2,1)} collective-permute-done((bf16[1088,384]{1,0:T(8,128)(2,1)S(1)}, bf16[1088,384]{1,0:T(8,128)(2,1)}, u32[]{:S(2)}, u32[]{:S(2)}) %collective-permute-start.20) | collective-permute-done | bytes 835616 | tf_op jit(solution)/shard_map/ppermute | solution.py:59
  773.3 2.9 copy.230
  793.0 2.9 copy.232
  (486 shorter events, 416.1 us)
Async XLA Ops:
  0.6 5.3 copy-start.63
  0.6 5.3 copy-start.35
  0.7 6.0 copy-start.27
  0.7 6.8 copy-start.19
  3.9 25.9 %collective-permute-start = (bf16[400,1152]{1,0:T(8,128)(2,1)}, bf16[400,1152]{1,0:T(8,128)(2,1)}, u32[]{:S(2)}, u32[]{:S(2)}) collective-permute-start(bf16[400,1152]{1,0:T(8,128)(2,1)} %fusion.83), channel_id=1, source_target_pairs={{0,16},{16,0},{1,17},{17,1},{2,18},{18,2},{3,19},{19,3},{4,20},{20... | collective-permute-start | bytes 2764808 | tf_op jit(solution)/shard_map/ppermute | solution.py:63
  10.3 51.1 %collective-permute-start.2 = (bf16[2128,384]{1,0:T(8,128)(2,1)}, bf16[2128,384]{1,0:T(8,128)(2,1)}, u32[]{:S(2)}, u32[]{:S(2)}) collective-permute-start(bf16[2128,384]{1,0:T(8,128)(2,1)} %constant_dynamic-update-slice_fusion), channel_id=1, source_target_pairs={{0,16},{16,0},{1,17},{17,1},{2,18},{18,2},{3,19},{19,3},{4,20},{20... | collective-permute-start | bytes 4902920 | tf_op jit(solution)/shard_map/ppermute | solution.py:63
  11.7 13.5 %copy-start.3 = (bf16[12,1024,64]{1,2,0:T(8,128)(2,1)}, bf16[12,1024,64]{1,2,0:T(8,128)(2,1)S(1)}, u32[]{:S(2)}) copy-start(bf16[12,1024,64]{1,2,0:T(8,128)(2,1)S(1)} %fusion.111) | copy-start | bytes 4718596
  16.1 6.1 copy-start.28
  27.8 6.2 copy-start.62
  28.1 50.2 %copy-start.49 = (f32[1024]{0:T(1024)}, f32[1024]{0:T(1024)S(1)}, u32[]{:S(2)}) copy-start(f32[1024]{0:T(1024)S(1)} %broadcast_multiply_fusion.1) | copy-start | bytes 12292
  29.8 56.9 %copy-start.36 = (f32[1024,32]{0,1:T(8,128)}, f32[1024,32]{0,1:T(8,128)S(1)}, u32[]{:S(2)}) copy-start(f32[1024,32]{0,1:T(8,128)S(1)} %get-tuple-element.381) | copy-start | bytes 393220
  29.8 40.7 %collective-permute-start.1 = (bf16[400,1152]{1,0:T(8,128)(2,1)}, bf16[400,1152]{1,0:T(8,128)(2,1)}, u32[]{:S(2)}, u32[]{:S(2)}) collective-permute-start(bf16[400,1152]{1,0:T(8,128)(2,1)} %collective-permute-done), channel_id=1, source_target_pairs={{0,1},{1,0},{2,3},{3,2},{4,5},{5,4},{6,7},{7,6},{8,9},{9,8},{10,11... | collective-permute-start | bytes 2764808 | tf_op jit(solution)/shard_map/ppermute | solution.py:59
  30.8 47.6 %copy-start.51 = (f32[1024]{0:T(1024)}, f32[1024]{0:T(1024)S(1)}, u32[]{:S(2)}) copy-start(f32[1024]{0:T(1024)S(1)} %fusion.94) | copy-start | bytes 12292
  34.1 44.3 %copy-start.53 = (f32[768]{0:T(1024)}, f32[768]{0:T(1024)S(1)}, u32[]{:S(2)}) copy-start(f32[768]{0:T(1024)S(1)} %fusion.96) | copy-start | bytes 9220
  68.5 155.8 %collective-permute-start.3 = (bf16[2128,384]{1,0:T(8,128)(2,1)}, bf16[2128,384]{1,0:T(8,128)(2,1)}, u32[]{:S(2)}, u32[]{:S(2)}) collective-permute-start(bf16[2128,384]{1,0:T(8,128)(2,1)} %collective-permute-done.2), channel_id=1, source_target_pairs={{0,1},{1,0},{2,3},{3,2},{4,5},{5,4},{6,7},{7,6},{8,9},{9,8},{10,11... | collective-permute-start | bytes 4902920 | tf_op jit(solution)/shard_map/ppermute | solution.py:59
  70.5 7.0 copy-start.16
  96.5 4.3 copy-start.7
  224.3 8.9 %copy-start.5 = (bf16[12,1024,64]{1,2,0:T(8,128)(2,1)}, bf16[12,1024,64]{1,2,0:T(8,128)(2,1)S(1)}, u32[]{:S(2)}) copy-start(bf16[12,1024,64]{1,2,0:T(8,128)(2,1)S(1)} %get-tuple-element.100) | copy-start | bytes 4718596
  230.3 2.9 copy-start.47
  233.2 3.0 copy-start.40
  234.8 5.0 copy-start.43
  235.2 5.4 copy-start.42
  244.2 3.1 copy-start.13
  244.2 3.2 copy-start.30
  247.4 4.3 copy-start.45
  247.4 4.3 copy-start.8
  247.4 4.3 copy-start.44
  247.4 4.3 copy-start.57
  266.7 4.5 copy-start.31
  282.7 9.7 %copy-start.23 = (f32[1024,768]{0,1:T(8,128)S(1)}, f32[1024,768]{0,1:T(8,128)}, u32[]{:S(2)}) copy-start(f32[1024,768]{0,1:T(8,128)} %get-tuple-element.386) | copy-start | bytes 9437188
  295.4 2.6 copy-start.34
  298.0 4.2 copy-start.4
  302.2 160.5 %copy-start.37 = (f32[1024,32]{0,1:T(8,128)S(1)}, f32[1024,32]{0,1:T(8,128)}, u32[]{:S(2)}) copy-start(f32[1024,32]{0,1:T(8,128)} %copy-done.36) | copy-start | bytes 393220
  302.2 160.5 %copy-start.39 = (f32[1024,32]{0,1:T(8,128)S(1)}, f32[1024,32]{0,1:T(8,128)}, u32[]{:S(2)}) copy-start(f32[1024,32]{0,1:T(8,128)} %get-tuple-element.382) | copy-start | bytes 393220
  467.7 4.9 copy-start.18
  467.8 4.8 copy-start.22
  476.4 7.1 copy-start.6
  483.6 33.6 %collective-permute-start.4 = (bf16[2,1152,384]{1,2,0:T(8,128)(2,1)}, bf16[2,1152,384]{1,2,0:T(8,128)(2,1)}, u32[]{:S(2)}, u32[]{:S(2)}) collective-permute-start(bf16[2,1152,384]{1,2,0:T(8,128)(2,1)} %pad_maximum_fusion), channel_id=1, source_target_pairs={{0,1},{1,0},{2,3},{3,2},{4,5},{5,4},{6,7},{7,6},{8,9},{9,8},{10,11... | collective-permute-start | bytes 5308424 | tf_op jit(solution)/shard_map/ppermute | solution.py:59
  486.4 9.7 %copy-start.9 = (bf16[1,1024,768]{1,2,0:T(8,128)(2,1)S(1)}, bf16[1,1024,768]{1,2,0:T(8,128)(2,1)}, u32[]{:S(2)}) copy-start(bf16[1,1024,768]{1,2,0:T(8,128)(2,1)} %copy.202) | copy-start | bytes 4718596
  486.4 9.7 %copy-start.58 = (pred[1024]{0:T(1024)(128)(4,1)S(1)}, pred[1024]{0:T(1024)(128)(4,1)}, u32[]{:S(2)}) copy-start(pred[1024]{0:T(1024)(128)(4,1)} %iota_compare_fusion.3) | copy-start | bytes 3076
  510.5 59.4 %collective-permute-start.13 = (bf16[2,2176,384]{1,2,0:T(8,128)(2,1)}, bf16[2,2176,384]{1,2,0:T(8,128)(2,1)}, u32[]{:S(2)}, u32[]{:S(2)}) collective-permute-start(bf16[2,2176,384]{1,2,0:T(8,128)(2,1)} %concatenate.218), channel_id=1, source_target_pairs={{0,1},{1,0},{2,3},{3,2},{4,5},{5,4},{6,7},{7,6},{8,9},{9,8},{10,11... | collective-permute-start | bytes 10027016 | tf_op jit(solution)/shard_map/ppermute | solution.py:59
  521.8 21.4 %collective-permute-start.5 = (bf16[1,1152,384]{1,2,0:T(8,128)(2,1)}, bf16[1,1152,384]{1,2,0:T(8,128)(2,1)}, u32[]{:S(2)}, u32[]{:S(2)}) collective-permute-start(bf16[1,1152,384]{1,2,0:T(8,128)(2,1)} %constant_dynamic-slice_fusion.22), channel_id=1, source_target_pairs={{0,16},{16,0},{1,17},{17,1},{2,18},{18,2},{3,19},{19,3},{4,20},{20... | collective-permute-start | bytes 2654216 | tf_op jit(solution)/shard_map/ppermute | solution.py:63
  546.7 19.4 %collective-permute-start.6 = (bf16[576,384]{0,1:T(8,128)(2,1)}, bf16[576,384]{0,1:T(8,128)(2,1)}, u32[]{:S(2)}, u32[]{:S(2)}) collective-permute-start(bf16[576,384]{0,1:T(8,128)(2,1)} %dynamic-slice_bitcast_fusion), channel_id=1, source_target_pairs={{0,2},{1,3},{2,0},{3,1},{4,6},{5,7},{6,4},{7,5},{8,10},{9,11},{10,... | collective-permute-start | bytes 1327112 | tf_op jit(solution)/shard_map/ppermute | solution.py:59
  568.6 9.3 %collective-permute-start.7 = (bf16[288,384]{0,1:T(8,128)(2,1)}, bf16[288,384]{0,1:T(8,128)(2,1)S(1)}, u32[]{:S(2)}, u32[]{:S(2)}) collective-permute-start(bf16[288,384]{0,1:T(8,128)(2,1)} %constant_dynamic-slice_fusion.21), channel_id=1, source_target_pairs={{0,4},{1,5},{2,6},{3,7},{4,0},{5,1},{6,2},{7,3},{8,12},{9,13},{10,... | collective-permute-start | bytes 663560 | tf_op jit(solution)/shard_map/ppermute | solution.py:59
  576.6 36.8 %collective-permute-start.14 = (bf16[1,2176,384]{1,2,0:T(8,128)(2,1)}, bf16[1,2176,384]{1,2,0:T(8,128)(2,1)}, u32[]{:S(2)}, u32[]{:S(2)}) collective-permute-start(bf16[1,2176,384]{1,2,0:T(8,128)(2,1)} %constant_dynamic-slice_fusion.13), channel_id=1, source_target_pairs={{0,16},{16,0},{1,17},{17,1},{2,18},{18,2},{3,19},{19,3},{4,20},{20... | collective-permute-start | bytes 5013512 | tf_op jit(solution)/shard_map/ppermute | solution.py:63
  579.1 34.3 %copy-start.11 = (bf16[2,2176,384]{1,2,0:T(8,128)(2,1)S(1)}, bf16[2,2176,384]{1,2,0:T(8,128)(2,1)}, u32[]{:S(2)}) copy-start(bf16[2,2176,384]{1,2,0:T(8,128)(2,1)} %copy-done.10) | copy-start | bytes 10027012
  579.1 12.2 %collective-permute-start.8 = (bf16[144,384]{0,1:T(8,128)(2,1)S(1)}, bf16[144,384]{0,1:T(8,128)(2,1)S(1)}, u32[]{:S(2)}, u32[]{:S(2)}) collective-permute-start(bf16[144,384]{0,1:T(8,128)(2,1)S(1)} %constant_dynamic-slice_fusion.20), channel_id=1, source_target_pairs={{0,8},{1,9},{2,10},{3,11},{4,12},{5,13},{6,14},{7,15},{8,0},{9,1},... | collective-permute-start | bytes 331784 | tf_op jit(solution)/shard_map/ppermute | solution.py:59
  591.5 35.9 %collective-permute-start.9 = (bf16[144,384]{0,1:T(8,128)(2,1)S(1)}, bf16[144,384]{0,1:T(8,128)(2,1)S(1)}, u32[]{:S(2)}, u32[]{:S(2)}) collective-permute-start(bf16[144,384]{0,1:T(8,128)(2,1)S(1)} %add_convert_fusion.12), channel_id=1, source_target_pairs={{0,8},{1,9},{2,10},{3,11},{4,12},{5,13},{6,14},{7,15},{8,0},{9,1},... | collective-permute-start | bytes 331784 | tf_op jit(solution)/shard_map/ppermute | solution.py:59
  620.0 7.7 copy-start.56
  620.0 7.7 copy-start.60
  620.0 18.1 %collective-permute-start.15 = (bf16[1088,384]{1,0:T(8,128)(2,1)}, bf16[1088,384]{1,0:T(8,128)(2,1)}, u32[]{:S(2)}, u32[]{:S(2)}) collective-permute-start(bf16[1088,384]{1,0:T(8,128)(2,1)} %bitcast.243), channel_id=1, source_target_pairs={{0,2},{1,3},{2,0},{3,1},{4,6},{5,7},{6,4},{7,5},{8,10},{9,11},{10,... | collective-permute-start | bytes 2506760 | tf_op jit(solution)/shard_map/ppermute | solution.py:59
  627.6 6.0 collective-permute-start.10
  634.8 18.8 %collective-permute-start.11 = (bf16[576,384]{0,1:T(8,128)(2,1)}, bf16[576,384]{0,1:T(8,128)(2,1)}, u32[]{:S(2)}, u32[]{:S(2)}) collective-permute-start(bf16[576,384]{0,1:T(8,128)(2,1)} %maximum_select_fusion.14), channel_id=1, source_target_pairs={{0,2},{1,3},{2,0},{3,1},{4,6},{5,7},{6,4},{7,5},{8,10},{9,11},{10,... | collective-permute-start | bytes 1327112 | tf_op jit(solution)/shard_map/ppermute | solution.py:59
  642.8 8.1 %collective-permute-start.16 = (bf16[544,384]{0,1:T(8,128)(2,1)S(1)}, bf16[544,384]{0,1:T(8,128)(2,1)S(1)}, u32[]{:S(2)}, u32[]{:S(2)}) collective-permute-start(bf16[544,384]{0,1:T(8,128)(2,1)S(1)} %constant_dynamic-slice_fusion.11), channel_id=1, source_target_pairs={{0,4},{1,5},{2,6},{3,7},{4,0},{5,1},{6,2},{7,3},{8,12},{9,13},{10,... | collective-permute-start | bytes 1253384 | tf_op jit(solution)/shard_map/ppermute | solution.py:59
  644.4 33.4 %copy-start.2 = (f32[1024,768]{0,1:T(8,128)S(1)}, f32[1024,768]{0,1:T(8,128)}, u32[]{:S(2)}) copy-start(f32[1024,768]{0,1:T(8,128)} %copy-done.1) | copy-start | bytes 9437188
  644.4 33.4 %copy-start.59 = (pred[1024]{0:T(1024)(128)(4,1)S(1)}, pred[1024]{0:T(1024)(128)(4,1)}, u32[]{:S(2)}) copy-start(pred[1024]{0:T(1024)(128)(4,1)} %iota_compare_fusion.3) | copy-start | bytes 3076
  651.4 15.5 %collective-permute-start.17 = (bf16[272,384]{0,1:T(8,128)(2,1)S(1)}, bf16[272,384]{0,1:T(8,128)(2,1)S(1)}, u32[]{:S(2)}, u32[]{:S(2)}) collective-permute-start(bf16[272,384]{0,1:T(8,128)(2,1)S(1)} %constant_dynamic-slice_fusion.10), channel_id=1, source_target_pairs={{0,8},{1,9},{2,10},{3,11},{4,12},{5,13},{6,14},{7,15},{8,0},{9,1},... | collective-permute-start | bytes 626696 | tf_op jit(solution)/shard_map/ppermute | solution.py:59
  656.5 78.1 %collective-permute-start.12 = (bf16[1152,384]{0,1:T(8,128)(2,1)}, bf16[1152,384]{0,1:T(8,128)(2,1)}, u32[]{:S(2)}, u32[]{:S(2)}) collective-permute-start(bf16[1152,384]{0,1:T(8,128)(2,1)} %maximum_select_fusion.8), channel_id=1, source_target_pairs={{0,1},{1,0},{2,3},{3,2},{4,5},{5,4},{6,7},{7,6},{8,9},{9,8},{10,11... | collective-permute-start | bytes 2654216 | tf_op jit(solution)/shard_map/ppermute | solution.py:59
  667.1 9.4 %collective-permute-start.18 = (bf16[272,384]{0,1:T(8,128)(2,1)S(1)}, bf16[272,384]{0,1:T(8,128)(2,1)S(1)}, u32[]{:S(2)}, u32[]{:S(2)}) collective-permute-start(bf16[272,384]{0,1:T(8,128)(2,1)S(1)} %add_convert_fusion.10), channel_id=1, source_target_pairs={{0,8},{1,9},{2,10},{3,11},{4,12},{5,13},{6,14},{7,15},{8,0},{9,1},... | collective-permute-start | bytes 626696 | tf_op jit(solution)/shard_map/ppermute | solution.py:59
  677.7 3.4 copy-start.61
  677.7 58.7 %collective-permute-start.19 = (bf16[544,384]{0,1:T(8,128)(2,1)}, bf16[544,384]{0,1:T(8,128)(2,1)}, u32[]{:S(2)}, u32[]{:S(2)}) collective-permute-start(bf16[544,384]{0,1:T(8,128)(2,1)} %maximum_select_fusion.15), channel_id=1, source_target_pairs={{0,4},{1,5},{2,6},{3,7},{4,0},{5,1},{6,2},{7,3},{8,12},{9,13},{10,... | collective-permute-start | bytes 1253384 | tf_op jit(solution)/shard_map/ppermute | solution.py:59
  681.1 3.7 copy-start.33
  739.8 19.8 %collective-permute-start.20 = (bf16[1088,384]{1,0:T(8,128)(2,1)S(1)}, bf16[1088,384]{1,0:T(8,128)(2,1)}, u32[]{:S(2)}, u32[]{:S(2)}) collective-permute-start(bf16[1088,384]{1,0:T(8,128)(2,1)S(1)} %copy.225), channel_id=1, source_target_pairs={{0,2},{1,3},{2,0},{3,1},{4,6},{5,7},{6,4},{7,5},{8,10},{9,11},{10,... | collective-permute-start | bytes 2506760 | tf_op jit(solution)/shard_map/ppermute | solution.py:59
  763.6 13.7 %collective-permute-start.21 = (bf16[2176,384]{0,1:T(8,128)(2,1)}, bf16[2176,384]{0,1:T(8,128)(2,1)}, u32[]{:S(2)}, u32[]{:S(2)}) collective-permute-start(bf16[2176,384]{0,1:T(8,128)(2,1)} %maximum_select_fusion.4), channel_id=1, source_target_pairs={{0,1},{1,0},{2,3},{3,2},{4,5},{5,4},{6,7},{7,6},{8,9},{9,8},{10,11... | collective-permute-start | bytes 5013512 | tf_op jit(solution)/shard_map/ppermute | solution.py:59
  (33 other events, 57.0 us)
